TPU v7x, 128 devices: a whole 4x4x4 slice. The times are simulated.
128 devices in a mesh: row: 16 (over y, z), col: 8 (over x, core).
Axes of the slice: x: 4, y: 4, z: 4, core: 2. Of those that a mesh axis runs over, the one named last changes fastest.
Arguments:
- grad_window: float32 [8192, 14336], P('row', 'col'), may hold values from -6 to 6
- rows_first: float32 [8192, 256], P('row'), may hold values from -0.0625 to 0.0625
- cols_first: float32 [14336, 256], P('col'), may hold values from -0.046875 to 0.046875
- rows_second: float32 [8192, 256], P('row'), may hold values from -0.0625 to 0.0625
- cols_second: float32 [14336, 256], P('col'), may hold values from -0.046875 to 0.046875
- inverse_first: float32 [256, 256], replicated, may hold values from -2 to 2, as said below
- inverse_second: float32 [256, 256], replicated, may hold values from -2 to 2, as said below
Outputs:
- panel_second: float32 [8192, 256], P('row')
- pivot_second: float32 [14336, 256], P('col')
- panel_first: float32 [8192, 256], P('row')
- pivot_first: float32 [14336, 256], P('col')
Inputs may be any that keep to these rules, and one draw needn't show every extreme that they name: `inverse_first`: lower triangular, diagonal entries between 1 and 2. `inverse_second`: lower triangular, diagonal entries between 1 and 2.
All inputs are finite; a program needn't handle non-finite values.
Results may differ from a plain program's by a relative error of at most 0.000071.
Values sent between devices are 32-bit elements; how exact they have to be, the bound alone decides.
No kernel may reach another device: no remote copies, remote signals or barrier semaphores. Data moves between devices by JAX's collectives and lax.ppermute only.
A program may use at most 64 MiB of HBM per device.

v0:
```python
import jax
import jax.numpy as jnp
from jax import lax
from jax.sharding import PartitionSpec as P


def matmul(left, right):
    return jnp.dot(left, right, precision=lax.Precision.HIGHEST, preferred_element_type=jnp.float32)


def tmatmul(left, right):
    return lax.dot_general(
        left,
        right,
        (((0,), (0,)), ((), ())),
        precision=lax.Precision.HIGHEST,
        preferred_element_type=jnp.float32,
    )


def local(
    grad_window, rows_first, cols_first, rows_second, cols_second, inverse_first, inverse_second
):
    col_count = lax.axis_size("col")
    is_last = lax.axis_index("col") == col_count - 1
    tile_cols = grad_window.shape[1]
    width = inverse_first.shape[0]
    left_sum = lax.psum(matmul(grad_window, cols_second), "col")
    panel_second = matmul(-left_sum, inverse_second)
    pivot_sum = lax.psum(tmatmul(grad_window, rows_second), "row")
    pivot_second = matmul(-pivot_sum, inverse_second)
    grad_next = grad_window.at[:, tile_cols - width :].add(jnp.where(is_last, panel_second, 0.0))
    left_next = lax.psum(matmul(grad_next, cols_first), "col")
    panel_first = matmul(-left_next, inverse_first)
    pivot_next = lax.psum(tmatmul(grad_next, rows_first), "row")
    pivot_first = matmul(-pivot_next, inverse_first)
    return (panel_second, pivot_second, panel_first, pivot_first)


def solution(mesh):
    in_specs = (
        P("row", "col"),
        P("row", None),
        P("col", None),
        P("row", None),
        P("col", None),
        P(),
        P(),
    )
    out_specs = (P("row", None), P("col", None), P("row", None), P("col", None))
    return jax.shard_map(local, mesh=mesh, in_specs=in_specs, out_specs=out_specs, check_vma=False)
```

profile of v0, /device:TPU:1, one launch (start us, length us, event | category | flops | bytes accessed | tf_op | source)
XLA Modules:
  0.0 263.9 jit_solution(18278489078048997041)
XLA Ops:
  7.2 0.0 copy-start
  7.2 0.0 all-reduce.5.cloned.1.call-start
  7.2 2.2 copy.17
  9.4 0.0 copy-start.1
  9.4 1.8 copy-done.1
  11.2 0.0 copy-done
  11.2 0.0 copy-start.6
  11.2 3.8 %fusion.8 = f32[512,256]{1,0:T(8,128)} fusion(f32[512,1792]{1,0:T(8,128)S(1)} %copy.17, f32[1792,256]{1,0:T(8,128)S(1)} %copy-done), kind=kOutput, calls=%fused_computation.9 | convolution fusion | flops 2818572288 | bytes 6029312 | tf_op jit(solution)/shard_map/dot_general | solution.py:8
  15.0 0.0 all-reduce.5.cloned.1.call-update
  15.1 0.2 all-reduce.7.cloned.1.call-start
  15.3 0.0 copy-done.6
  15.3 0.0 copy-start.4
  15.3 9.2 %fusion.9 = f32[1792,256]{1,0:T(8,128)} fusion(f32[512,1792]{1,0:T(8,128)} %copy-done.1, f32[512,256]{1,0:T(8,128)S(1)} %copy-done.6), kind=kOutput, calls=%fused_computation.10 | convolution fusion | flops 2818572288 | bytes 6029312 | tf_op jit(solution)/shard_map/dot_general | solution.py:12
  24.5 52.4 %all-reduce.5.cloned.1.call-done = f32[512,256]{1,0:T(8,128)} async-done(((f32[512,256]{1,0:T(8,128)}), f32[512,256]{1,0:T(8,128)}) %all-reduce.5.cloned.1.call-update) | async-done | bytes 524304 | tf_op jit(solution)/shard_map/psum | solution.py:28
  77.0 0.0 copy-done.4
  77.0 0.0 copy-start.2
  77.0 2.9 %add_dynamic-update-slice_fusion = (f32[512,1792]{1,0:T(8,128)}, f32[512,256]{1,0:T(8,128)}) fusion(f32[512,1792]{1,0:T(8,128)} %copy-done.1, pred[]{:T(512)S(6)} %eq.3, f32[256,256]{1,0:T(8,128)S(1)} %copy-done.4, f32[512,256]{1,0:T(8,128)} %all-reduce.5.cloned.1.call-done), kind=kOutput, calls=%fused_computation.6 | convolution fusion | flops 403046400 | bytes 2359297 | tf_op jit(solution)/shard_map/dot_general | solution.py:8
  79.9 0.0 copy-done.2
  79.9 0.0 copy-start.7
  79.9 5.9 %fusion.10 = f32[512,256]{1,0:T(8,128)} fusion(f32[512,1792]{1,0:T(8,128)} %get-tuple-element.18, f32[1792,256]{1,0:T(8,128)S(1)} %copy-done.2), kind=kOutput, calls=%fused_computation.11 | convolution fusion | flops 2818572288 | bytes 6029312 | tf_op jit(solution)/shard_map/dot_general | solution.py:8
  85.8 0.0 all-reduce.7.cloned.1.call-update
  85.9 0.3 all-reduce.9.cloned.1.call-start
  86.1 0.0 copy-done.7
  86.1 9.1 %fusion.11 = f32[1792,256]{1,0:T(8,128)} fusion(f32[512,1792]{1,0:T(8,128)} %get-tuple-element.18, f32[512,256]{1,0:T(8,128)S(1)} %copy-done.7), kind=kOutput, calls=%fused_computation.12 | convolution fusion | flops 2818572288 | bytes 6029312 | tf_op jit(solution)/shard_map/dot_general | solution.py:12
  95.3 0.0 all-reduce.9.cloned.1.call-update
  95.3 50.5 %all-reduce.7.cloned.1.call-done = f32[512,256]{1,0:T(8,128)} async-done(((f32[512,256]{1,0:T(8,128)}), f32[512,256]{1,0:T(8,128)}) %all-reduce.7.cloned.1.call-update) | async-done | bytes 524304 | tf_op jit(solution)/shard_map/psum | solution.py:33
  145.8 0.0 copy-done.5
  145.8 2.4 fusion.4
  148.2 101.8 %all-reduce.9.cloned.1.call-done = (f32[1792,256]{1,0:T(8,128)}, f32[1792,256]{1,0:T(8,128)}) async-done(((f32[1792,256]{1,0:T(8,128)}, f32[1792,256]{1,0:T(8,128)}), (f32[1792,256]{1,0:T(8,128)}, f32[1792,256]{1,0:T(8,128)})) %all-reduce.9.cloned.1.call-update) | async-done | bytes 3670032 | tf_op jit(solution)/shard_map/psum | solution.py:30
  250.1 4.5 %fusion.2 = f32[1792,256]{1,0:T(8,128)} fusion(f32[256,256]{1,0:T(8,128)S(1)} %copy-done.4, f32[1792,256]{1,0:T(8,128)} %get-tuple-element.16), kind=kOutput, calls=%fused_computation.2 | convolution fusion | flops 1409744896 | bytes 3932160 | tf_op jit(solution)/shard_map/dot_general | solution.py:8
  254.5 0.0 copy-done.3
  254.5 2.8 %fusion = f32[1792,256]{1,0:T(8,128)} fusion(f32[256,256]{1,0:T(8,128)S(1)} %copy-done.5, f32[1792,256]{1,0:T(8,128)S(1)} %copy-done.3), kind=kOutput, calls=%fused_computation | convolution fusion | flops 1409744896 | bytes 3932160 | tf_op jit(solution)/shard_map/dot_general | solution.py:8
  (2 shorter events, 0.0 us)
Async XLA Ops:
  7.2 4.0 %copy-start = (f32[1792,256]{1,0:T(8,128)S(1)}, f32[1792,256]{1,0:T(8,128)}, u32[]{:S(2)}) copy-start(f32[1792,256]{1,0:T(8,128)} %param.13) | copy-start | bytes 5505028
  7.2 69.8 %all-reduce.5.cloned.1.call-start = ((), (), s32[]{:S(2)}) async-start(), calls=%async_computation | async-start | bytes 1048576 | tf_op jit(solution)/shard_map/psum | solution.py:28
  9.4 1.8 copy-start.1
  11.2 4.1 %copy-start.6 = (f32[512,256]{1,0:T(8,128)S(1)}, f32[512,256]{1,0:T(8,128)}, u32[]{:S(2)}) copy-start(f32[512,256]{1,0:T(8,128)} %param.12) | copy-start | bytes 1572868
  15.1 130.7 %all-reduce.7.cloned.1.call-start = ((), (), s32[]{:S(2)}) async-start(), calls=%async_computation.1 | async-start | bytes 1048576 | tf_op jit(solution)/shard_map/psum | solution.py:33
  15.3 61.6 %copy-start.4 = (f32[256,256]{1,0:T(8,128)S(1)}, f32[256,256]{1,0:T(8,128)}, u32[]{:S(2)}) copy-start(f32[256,256]{1,0:T(8,128)} %param.15) | copy-start | bytes 786436
  77.0 2.9 %copy-start.2 = (f32[1792,256]{1,0:T(8,128)S(1)}, f32[1792,256]{1,0:T(8,128)}, u32[]{:S(2)}) copy-start(f32[1792,256]{1,0:T(8,128)} %param.11) | copy-start | bytes 5505028
  79.9 6.2 %copy-start.7 = (f32[512,256]{1,0:T(8,128)S(1)}, f32[512,256]{1,0:T(8,128)}, u32[]{:S(2)}) copy-start(f32[512,256]{1,0:T(8,128)} %param.10) | copy-start | bytes 1572868
  85.9 164.2 %all-reduce.9.cloned.1.call-start = ((), (), s32[]{:S(2)}) async-start(), calls=%async_computation.2 | async-start | bytes 7340032 | tf_op jit(solution)/shard_map/psum | solution.py:30
  95.3 50.5 %copy-start.5 = (f32[256,256]{1,0:T(8,128)S(1)}, f32[256,256]{1,0:T(8,128)}, u32[]{:S(2)}) copy-start(f32[256,256]{1,0:T(8,128)} %param.14) | copy-start | bytes 786436
  250.1 4.5 %copy-start.3 = (f32[1792,256]{1,0:T(8,128)S(1)}, f32[1792,256]{1,0:T(8,128)}, u32[]{:S(2)}) copy-start(f32[1792,256]{1,0:T(8,128)} %get-tuple-element.17) | copy-start | bytes 5505028
Sparse Core Ops, SparseCore 0:
  15.2 61.7 all-reduce.4
  86.0 59.7 all-reduce.6
  149.8 100.1 all-reduce.8
where the time goes:
time: 264 us
  waiting for transfers between devices  205 us (78%)
  matrix products  40.8 us (15%)
  between operations  13.8 us (5%)
  local copies, waits for them, and re-layouts  4 us (2%)
    psum x1, waiting for transfers between devices, local(): pivot_sum = lax.psum(tmatmul(grad_window, rows_second), 'row')  102 us
    psum x1, waiting for transfers between devices, local(): left_sum = lax.psum(matmul(grad_window, cols_second), 'col')  52.4 us
    psum x1, waiting for transfers between devices, local(): left_next = lax.psum(matmul(grad_next, cols_first), 'col')  50.5 us
    dot_general x6, matrix products, matmul(): jnp.dot(left, right, precision=lax.Precision.HIGHEST, preferred_element_t...  22.4 us
    dot_general x2, matrix products, tmatmul(): lax.dot_general(left, right, (((0,), (0,)), ((), ())), precision=lax.Prec...  18.3 us
  transfers between devices with their start and end apart: 3, of which 3 were waited for; matrix products, arithmetic and copies ran while one was open for 8% of the time, Pallas kernels for 0%

commit v1 on v0

--- a/solution.py
+++ b/solution.py
@@ -30,7 +30,7 @@
     pivot_sum = lax.psum(tmatmul(grad_window, rows_second), "row")
     pivot_second = matmul(-pivot_sum, inverse_second)
     grad_next = grad_window.at[:, tile_cols - width :].add(jnp.where(is_last, panel_second, 0.0))
-    left_next = lax.psum(matmul(grad_next, cols_first), "col")
+    left_next = jnp.sum(lax.all_gather(matmul(grad_next, cols_first), "col"), axis=0)
     panel_first = matmul(-left_next, inverse_first)
     pivot_next = lax.psum(tmatmul(grad_next, rows_first), "row")
     pivot_first = matmul(-pivot_next, inverse_first)

time: 264 us -> 235 us (0.89)
  waiting for transfers between devices: 205 us -> 174 us
    psum x1 -> x0, waiting for transfers between devices: 50.5 us -> none  [local(): left_next = lax.psum(matmul(grad_next, cols_first), 'col')]
    all_gather x0 -> x1, waiting for transfers between devices: none -> 27.3 us  [local(): lax.all_gather(matmul(grad_next, cols_first), 'col')]
    psum x1, waiting for transfers between devices: 102 us -> 93.8 us  [local(): pivot_sum = lax.psum(tmatmul(grad_window, rows_second), 'row')]
  transfers between devices with their start and end apart: 3 -> 3, of which waited for: 3 -> 3; matrix products, arithmetic and copies ran while one was open for 8% -> 10% of each run, Pallas kernels for 0% -> 0%
where the time goes in v1:
time: 235 us; the launch traced here: 234 us
  waiting for transfers between devices  174 us (74%)
  matrix products  40.3 us (17%)
  between operations  13.8 us (6%)
  local copies, waits for them, and re-layouts  4 us (2%)
  other arithmetic  2.52 us (1%)
    psum x1, waiting for transfers between devices, local(): pivot_sum = lax.psum(tmatmul(grad_window, rows_second), 'row')  93.8 us
    psum x1, waiting for transfers between devices, local(): left_sum = lax.psum(matmul(grad_window, cols_second), 'col')  52.4 us
    all_gather x1, waiting for transfers between devices, local(): lax.all_gather(matmul(grad_next, cols_first), 'col')  27.3 us
    dot_general x6, matrix products, matmul(): jnp.dot(left, right, precision=lax.Precision.HIGHEST, preferred_element_t...  21.8 us
    dot_general x2, matrix products, tmatmul(): lax.dot_general(left, right, (((0,), (0,)), ((), ())), precision=lax.Prec...  18.6 us
  transfers between devices with their start and end apart: 3, of which 3 were waited for; matrix products, arithmetic and copies ran while one was open for 10% of the time, Pallas kernels for 0%

profile of v1, /device:TPU:1, one launch (start us, length us, event | category | flops | bytes accessed | tf_op | source)
XLA Modules:
  0.0 234.5 jit_solution(11741947588229543372)
XLA Ops:
  7.2 0.0 copy-start
  7.2 0.0 all-reduce.4.cloned.1.call-start
  7.2 2.2 copy.16
  9.4 0.0 copy-start.1
  9.4 1.8 copy-done.1
  11.2 0.0 copy-done
  11.2 0.0 copy-start.5
  11.2 3.8 %fusion.8 = f32[512,256]{1,0:T(8,128)} fusion(f32[512,1792]{1,0:T(8,128)S(1)} %copy.16, f32[1792,256]{1,0:T(8,128)S(1)} %copy-done), kind=kOutput, calls=%fused_computation.9 | convolution fusion | flops 2818572288 | bytes 6029312 | tf_op jit(solution)/shard_map/dot_general | solution.py:8
  15.0 0.0 all-reduce.4.cloned.1.call-update
  15.1 0.2 all-reduce.6.cloned.1.call-start
  15.3 0.0 copy-done.5
  15.3 0.0 copy-start.3
  15.3 9.2 %fusion.9 = f32[1792,256]{1,0:T(8,128)} fusion(f32[512,1792]{1,0:T(8,128)} %copy-done.1, f32[512,256]{1,0:T(8,128)S(1)} %copy-done.5), kind=kOutput, calls=%fused_computation.10 | convolution fusion | flops 2818572288 | bytes 6029312 | tf_op jit(solution)/shard_map/dot_general | solution.py:12
  24.5 0.0 copy-start.6
  24.5 52.4 %all-reduce.4.cloned.1.call-done = f32[512,256]{1,0:T(8,128)} async-done(((f32[512,256]{1,0:T(8,128)}), f32[512,256]{1,0:T(8,128)}) %all-reduce.4.cloned.1.call-update) | async-done | bytes 524304 | tf_op jit(solution)/shard_map/psum | solution.py:28
  77.0 0.0 copy-done.3
  77.0 2.8 %add_dynamic-update-slice_fusion = (f32[512,1792]{1,0:T(8,128)}, f32[512,256]{1,0:T(8,128)}) fusion(f32[512,1792]{1,0:T(8,128)} %copy-done.1, pred[]{:T(512)S(6)} %eq.3, f32[256,256]{1,0:T(8,128)S(1)} %copy-done.3, f32[512,256]{1,0:T(8,128)} %all-reduce.4.cloned.1.call-done), kind=kOutput, calls=%fused_computation.6 | convolution fusion | flops 403046400 | bytes 2359297 | tf_op jit(solution)/shard_map/dot_general | solution.py:8
  79.8 0.0 copy-done.6
  79.8 9.4 %fusion.11 = f32[1792,256]{1,0:T(8,128)} fusion(f32[512,1792]{1,0:T(8,128)} %get-tuple-element.18, f32[512,256]{1,0:T(8,128)S(1)} %copy-done.6), kind=kOutput, calls=%fused_computation.12 | convolution fusion | flops 2818572288 | bytes 6029312 | tf_op jit(solution)/shard_map/dot_general | solution.py:12
  89.1 0.0 all-reduce.6.cloned.1.call-update
  89.2 0.0 all-gather.3.cloned.1.call-start
  89.2 6.4 %fusion.10 = f32[512,256]{1,0:T(8,128)} fusion(f32[512,1792]{1,0:T(8,128)} %get-tuple-element.18, f32[1792,256]{1,0:T(8,128)} %param.11), kind=kOutput, calls=%fused_computation.11 | convolution fusion | flops 2818572288 | bytes 6029312 | tf_op jit(solution)/shard_map/dot_general | solution.py:8
  95.6 0.0 all-gather.3.cloned.1.call-update
  95.7 93.8 %all-reduce.6.cloned.1.call-done = (f32[1792,256]{1,0:T(8,128)}, f32[1792,256]{1,0:T(8,128)}) async-done(((f32[1792,256]{1,0:T(8,128)}, f32[1792,256]{1,0:T(8,128)}), (f32[1792,256]{1,0:T(8,128)}, f32[1792,256]{1,0:T(8,128)})) %all-reduce.6.cloned.1.call-update) | async-done | bytes 3670032 | tf_op jit(solution)/shard_map/psum | solution.py:30
  189.5 0.0 copy-start.2
  189.5 4.5 %fusion.2 = f32[1792,256]{1,0:T(8,128)} fusion(f32[256,256]{1,0:T(8,128)S(1)} %copy-done.3, f32[1792,256]{1,0:T(8,128)} %get-tuple-element.16), kind=kOutput, calls=%fused_computation.2 | convolution fusion | flops 1409744896 | bytes 3932160 | tf_op jit(solution)/shard_map/dot_general | solution.py:8
  194.0 0.0 copy-done.2
  194.0 0.0 copy-done.4
  194.0 2.8 %fusion = f32[1792,256]{1,0:T(8,128)} fusion(f32[256,256]{1,0:T(8,128)S(1)} %copy-done.4, f32[1792,256]{1,0:T(8,128)S(1)} %copy-done.2), kind=kOutput, calls=%fused_computation | convolution fusion | flops 1409744896 | bytes 3932160 | tf_op jit(solution)/shard_map/dot_general | solution.py:8
  196.8 27.3 %all-gather.3.cloned.1.call-done = f32[4096,256]{1,0:T(8,128)} async-done(((f32[512,256]{1,0:T(8,128)}), f32[4096,256]{1,0:T(8,128)}) %all-gather.3.cloned.1.call-update) | async-done | bytes 4194320 | tf_op jit(solution)/shard_map/all_gather | solution.py:33
  224.1 2.5 %reduce_sum.9 = f32[512,256]{1,0:T(8,128)S(1)} reduce(f32[8,512,256]{2,1,0:T(8,128)} %bitcast.13, f32[]{:T(128)} %constant.35.clone.1), dimensions={0}, to_apply=%region_2.3 | reduce | flops 917504 | bytes 4718596 | tf_op jit(solution)/shard_map/reduce_sum | solution.py:33
  226.6 1.4 fusion.4
  (1 shorter events, 0.0 us)
Async XLA Ops:
  7.2 4.0 %copy-start = (f32[1792,256]{1,0:T(8,128)S(1)}, f32[1792,256]{1,0:T(8,128)}, u32[]{:S(2)}) copy-start(f32[1792,256]{1,0:T(8,128)} %param.13) | copy-start | bytes 5505028
  7.2 69.8 %all-reduce.4.cloned.1.call-start = ((), (), s32[]{:S(2)}) async-start(), calls=%async_computation | async-start | bytes 1048576 | tf_op jit(solution)/shard_map/psum | solution.py:28
  9.4 1.8 copy-start.1
  11.2 4.1 %copy-start.5 = (f32[512,256]{1,0:T(8,128)S(1)}, f32[512,256]{1,0:T(8,128)}, u32[]{:S(2)}) copy-start(f32[512,256]{1,0:T(8,128)} %param.12) | copy-start | bytes 1572868
  15.1 174.4 %all-reduce.6.cloned.1.call-start = ((), (), s32[]{:S(2)}) async-start(), calls=%async_computation.2 | async-start | bytes 7340032 | tf_op jit(solution)/shard_map/psum | solution.py:30
  15.3 61.6 %copy-start.3 = (f32[256,256]{1,0:T(8,128)S(1)}, f32[256,256]{1,0:T(8,128)}, u32[]{:S(2)}) copy-start(f32[256,256]{1,0:T(8,128)} %param.15) | copy-start | bytes 786436
  24.5 55.2 %copy-start.6 = (f32[512,256]{1,0:T(8,128)S(1)}, f32[512,256]{1,0:T(8,128)}, u32[]{:S(2)}) copy-start(f32[512,256]{1,0:T(8,128)} %param.10) | copy-start | bytes 1572868
  89.2 134.9 %all-gather.3.cloned.1.call-start = ((), (), s32[]{:S(2)}) async-start(), calls=%async_computation.1 | async-start | bytes 4718592 | tf_op jit(solution)/shard_map/all_gather | solution.py:33
  189.5 4.5 %copy-start.2 = (f32[1792,256]{1,0:T(8,128)S(1)}, f32[1792,256]{1,0:T(8,128)}, u32[]{:S(2)}) copy-start(f32[1792,256]{1,0:T(8,128)} %get-tuple-element.17) | copy-start | bytes 5505028
  189.5 4.5 %copy-start.4 = (f32[256,256]{1,0:T(8,128)S(1)}, f32[256,256]{1,0:T(8,128)}, u32[]{:S(2)}) copy-start(f32[256,256]{1,0:T(8,128)} %param.14) | copy-start | bytes 786436
Sparse Core Ops, SparseCore 0:
  15.2 61.7 all-reduce.3
  89.3 100.1 all-reduce.5
  191.9 32.1 all-gather.2
